TPU v7x, 128 devices: a whole 4x4x4 slice. The times are simulated.
128 devices in a mesh: adapter: 32 (over y, x, core), mp: 4 (over z).
Axes of the slice: x: 4, y: 4, z: 4, core: 2. Of those that a mesh axis runs over, the one named last changes fastest.
Arguments:
- hidden: bfloat16 [8192, 4096], P('adapter', 'mp'), may hold values from -8 to 8
- subsets: int32 [8192, 8], P('adapter'), may hold values from 0 to 31, all different within a row; in each aligned block of 256 rows (0 to 255, 256 to 511, ...) at most 128 rows name the same one
- down_weight: bfloat16 [32, 4096, 256], P('adapter', 'mp'), may hold values from -0.09375 to 0.09375
- up_weight: bfloat16 [32, 256, 4096], P('adapter', None, 'mp'), may hold values from -0.375 to 0.375
- query_weight: bfloat16 [4096, 4096], P('mp'), may hold values from -0.08 to 2.08
- key_weight: bfloat16 [4096, 4096], P('mp'), may hold values from -0.08 to 2.08
Outputs:
- joined: bfloat16 [8192, 4096], P('adapter', 'mp')
Inputs may be any that keep to these rules, and one draw needn't show every extreme that they name: `subsets`: each row names 8 different adapters; within the rows of one index of the adapter axis no adapter is named by more than 128 rows.
All inputs are finite; a program needn't handle non-finite values.
Results may differ from a plain program's by a relative error of at most 0.025.
Values may be sent and summed in bfloat16 or wider, within the bound.
No kernel may reach another device: no remote copies, remote signals or barrier semaphores. Data moves between devices by JAX's collectives and lax.ppermute only.
A program may use at most 192 MiB of HBM per device.

v0:
```python
import jax
import jax.numpy as jnp
from jax import lax
from jax.sharding import PartitionSpec as P

D = 4096


def sent_to_all(x, axis):
    size = lax.axis_size(axis)
    return lax.all_to_all(jnp.broadcast_to(x[None], (size, *x.shape)), axis, 0, 0, tiled=True)


def over_copies(x, axis):
    return sent_to_all(x, axis).astype(jnp.float32).sum(axis=0)


def split_up(x, dim, size):
    before, after = (x.shape[:dim], x.shape[dim + 1 :])
    return jnp.moveaxis(x.reshape(*before, size, -1, *after), dim, 0)


def sent_and_summed(x, axis, dim):
    size = lax.axis_size(axis)
    parts = lax.all_to_all(split_up(x, dim, size), axis, 0, 0, tiled=True)
    return jnp.sum(parts.astype(jnp.float32), axis=0)


def in_order(parts, dim):
    parts = jnp.moveaxis(parts, 0, dim)
    shape = parts.shape
    return parts.reshape(*shape[:dim], shape[dim] * shape[dim + 1], *shape[dim + 2 :])


def collect(x, axis, dim):
    parts = sent_to_all(x, axis)
    return in_order(parts, dim)


def taken_together(x, axis):
    return sent_to_all(x, axis).sum(axis=0)


def tally(partial_sum):
    summed = over_copies(partial_sum.astype(jnp.bfloat16), "mp").astype(jnp.float32)
    return jnp.maximum(summed, 0.0).astype(jnp.bfloat16)


def per_device(hidden, subsets, down_weight, up_weight, query_weight, key_weight):
    row_count, width_local = hidden.shape
    fanout = subsets.shape[1]
    total_adapters = lax.axis_size("adapter") * down_weight.shape[0]
    capacity = min(row_count, 2 * row_count * fanout // total_adapters)
    labels = jnp.arange(total_adapters, dtype=jnp.int32)
    picks = (subsets[:, :, None] == labels[None, None, :]).astype(jnp.int32)
    chosen = jnp.sum(picks, axis=1)
    before = jnp.cumsum(chosen, axis=0) - chosen
    slot_rank = jnp.sum(picks * before[:, None, :], axis=2)
    flat_slot = subsets * capacity + slot_rank
    row_ids = jnp.broadcast_to(jnp.arange(row_count, dtype=jnp.int32)[:, None], flat_slot.shape)
    source_row = (
        jnp.zeros((total_adapters * capacity,), jnp.int32)
        .at[flat_slot.reshape(-1)]
        .set(row_ids.reshape(-1))
    )
    filled = jnp.zeros((total_adapters * capacity,), jnp.bool_).at[flat_slot.reshape(-1)].set(True)
    outgoing = jnp.where(
        filled[:, None], jnp.take(hidden, source_row, axis=0), jnp.zeros((), jnp.bfloat16)
    )
    outgoing = outgoing.reshape(total_adapters, capacity, width_local)
    query_part = jnp.dot(hidden, query_weight, preferred_element_type=jnp.float32)
    query_piece = sent_and_summed(query_part.astype(jnp.bfloat16), "mp", 1).astype(jnp.bfloat16)
    query = collect(query_piece, "mp", 1)
    probe = lax.dot_general(
        query, key_weight, (((1,), (1,)), ((), ())), preferred_element_type=jnp.float32
    ).astype(jnp.bfloat16)
    block = outgoing
    bottle = tally(
        jnp.einsum(
            "ncd,ndb->ncb",
            block,
            lax.all_gather(down_weight, "adapter", axis=0, tiled=True),
            preferred_element_type=jnp.float32,
        )
    )
    block = bottle
    returned = jnp.einsum(
        "ncb,nbd->ncd",
        block,
        lax.all_gather(up_weight, "adapter", axis=0, tiled=True),
        preferred_element_type=jnp.float32,
    ).astype(jnp.bfloat16)
    picked = jnp.take(returned.reshape(total_adapters * capacity, width_local), flat_slot, axis=0)
    widened = picked.astype(jnp.float32)
    base = hidden.astype(jnp.float32)
    probe_wide = probe.astype(jnp.float32)
    own_term = jnp.sum(base * probe_wide, axis=1)
    partial_logit = (
        jnp.einsum("rkd,rd->rk", widened, probe_wide, precision=lax.Precision.HIGHEST)
        + own_term[:, None]
    )
    logits = taken_together(partial_logit, "mp") * D ** (-0.5)
    share = jax.nn.softmax(logits, axis=-1)
    joined = base + jnp.einsum("rk,rkd->rd", share, widened, precision=lax.Precision.HIGHEST)
    return joined.astype(jnp.bfloat16)


def solution(mesh):
    return jax.shard_map(
        per_device,
        mesh=mesh,
        in_specs=(
            P("adapter", "mp"),
            P("adapter", None),
            P("adapter", "mp", None),
            P("adapter", None, "mp"),
            P("mp", None),
            P("mp", None),
        ),
        out_specs=P("adapter", "mp"),
        check_vma=False,
    )
```

profile of v0, /device:TPU:0, one launch (start us, length us, event | category | flops | bytes accessed | tf_op | source)
XLA Modules:
  0.0 257.7 jit_solution(9191249026218513655)
XLA Ops:
  6.5 0.0 all-gather.3.cloned.1.call-start
  6.5 0.7 all-gather.3.cloned.1.call-update
  7.3 0.0 all-gather.5.cloned.1.call-start
  7.3 0.7 all-gather.5.cloned.1.call-update
  8.0 5.9 %convolution_convert_fusion.1 = bf16[256,4096]{1,0:T(8,128)(2,1)S(1)} fusion(bf16[256,1024]{1,0:T(8,128)(2,1)} %param.6, bf16[1024,4096]{1,0:T(8,128)(2,1)} %param.10), kind=kOutput, calls=%fused_computation.11 | convolution fusion | flops 2148532224 | bytes 11010048 | tf_op jit(solution)/shard_map/dot_general | solution.py:71
  13.9 0.0 copy-start.1
  13.9 0.0 copy-start
  13.9 1.6 copy.58
  15.5 5.4 %all-to-all-start.1 = ((bf16[4,256,1024]{2,1,0:T(8,128)(2,1)}), bf16[4,256,1024]{2,1,0:T(8,128)(2,1)S(1)}, u32[]{:S(2)}, u32[]{:S(2)}) async-start(bf16[4,256,1024]{2,1,0:T(8,128)(2,1)} %bitcast.53), calls=%async_computation.1 | async-start | bytes 4194304 | tf_op jit(solution)/shard_map/all_to_all | solution.py:25
  20.9 0.0 copy-done.1
  21.0 0.6 reduce-window.6
  21.5 0.2 slice_reduce_fusion
  21.8 0.1 fusion.18
  21.9 0.1 select_reduce_fusion
  21.9 0.1 copy.39
  22.1 0.1 reshape.87
  22.2 0.1 reshape.120
  22.3 8.1 %scatter_custom_fusion.1 = s32[4096]{0:T(1024)S(1)} fusion(s32[2048]{0:T(1024)S(1)} %bitcast.55, s32[2048]{0:T(1024)S(1)} %reshape.120, s32[]{:T(128)} %constant.18.clone.1), kind=kCustom, calls=%fused_computation.45 | custom fusion | bytes 16388 | tf_op jit(solution)/shard_map/scatter | solution.py:64
  30.4 0.0 copy-done
  30.4 18.2 %gather_fusion = bf16[4096,1024]{1,0:T(8,128)(2,1)} fusion(bf16[256,1024]{1,0:T(8,128)(2,1)S(1)} %copy-done, s32[4096]{0:T(1024)S(1)} %fusion.19), kind=kCustom, calls=%fused_computation | custom fusion | bytes 16793600 | tf_op jit(solution)/shard_map/jit(_take)/gather | solution.py:68
  48.7 9.1 %scatter_custom_fusion = pred[4096]{0:T(1024)(128)(4,1)S(1)} fusion(s32[2048]{0:T(1024)S(1)} %bitcast.56, pred[2048]{0:T(1024)(128)(4,1)S(1)} %broadcast.50, pred[]{:T(512)} %constant.27.clone.1), kind=kCustom, calls=%fused_computation.48 | custom fusion | bytes 4097 | tf_op jit(solution)/shard_map/scatter | solution.py:66
  57.8 0.0 all-to-all-done.1
  57.8 0.4 reduce_sum.69
  58.2 0.2 copy.43
  58.4 1.4 broadcast_in_dim.97
  59.9 4.8 %all-to-all-start.2 = ((bf16[4,256,1024]{1,2,0:T(8,128)(2,1)}), bf16[4,256,1024]{1,2,0:T(8,128)(2,1)}, u32[]{:S(2)}, u32[]{:S(2)}) async-start(bf16[4,256,1024]{1,2,0:T(8,128)(2,1)} %broadcast_in_dim.97), calls=%async_computation.2 | async-start | bytes 4194304 | tf_op jit(solution)/shard_map/all_to_all | solution.py:11
  64.7 19.8 %all-gather.3.cloned.1.call-done = bf16[32,1024,256]{2,1,0:T(8,128)(2,1)} async-done(((bf16[1,1024,256]{2,1,0:T(8,128)(2,1)}), bf16[32,1024,256]{2,1,0:T(8,128)(2,1)}) %all-gather.3.cloned.1.call-update) | async-done | bytes 16777232 | tf_op jit(solution)/shard_map/all_gather | solution.py:82
  84.5 9.7 %fusion.12 = bf16[32,128,256]{2,1,0:T(8,128)(2,1)S(1)} fusion(bf16[32,1024,256]{2,1,0:T(8,128)(2,1)} %all-gather.3.cloned.1.call-done, bf16[32,128,1024]{2,1,0:T(8,128)(2,1)} %bitcast.52, pred[32,128]{1,0:T(8,128)(4,1)S(1)} %and_bitcast_fusion, pred[32,128]{1,0:T(8,128)(4,1)S(1)} %bitcast.57), kind=kOutput, calls=%fused_computation.22 | convolution fusion | flops 2156920832 | bytes 27271168 | tf_op jit(solution)/shard_map/ncd,ndb->ncb/dot_general | solution.py:79
  94.2 0.0 all-to-all-done.2
  94.2 4.3 %broadcast_in_dim.94 = bf16[4,32,128,256]{3,2,1,0:T(8,128)(2,1)} broadcast(bf16[32,128,256]{2,1,0:T(8,128)(2,1)S(1)} %fusion.12), dimensions={1,2,3} | broadcast | bytes 10485760 | tf_op jit(solution)/shard_map/broadcast_in_dim | solution.py:11
  98.4 5.8 %all-to-all-start = ((bf16[4,32,128,256]{3,2,1,0:T(8,128)(2,1)}), bf16[4,32,128,256]{3,2,1,0:T(8,128)(2,1)}, u32[]{:S(2)}, u32[]{:S(2)}) async-start(bf16[4,32,128,256]{3,2,1,0:T(8,128)(2,1)} %broadcast_in_dim.94), calls=%async_computation | async-start | bytes 16777216 | tf_op jit(solution)/shard_map/all_to_all | solution.py:11
  104.3 0.1 copy.40
  104.4 0.1 reshape.102
  104.5 0.2 copy.38
  104.7 6.5 %fusion.15 = (f32[256]{0:T(256)S(1)}, bf16[256,1024]{1,0:T(8,128)(2,1)S(1)}) fusion(bf16[256,1024]{1,0:T(8,128)(2,1)S(1)} %copy-done, bf16[256,4096]{0,1:T(8,128)(2,1)} %bitcast.10, bf16[1024,4096]{1,0:T(8,128)(2,1)} %param.11), kind=kOutput, calls=%fused_computation.26 | convolution fusion | flops 2148794112 | bytes 11535360 | tf_op jit(solution)/shard_map/dot_general | solution.py:74
  111.3 87.5 %all-to-all-done = bf16[4,32,128,256]{3,2,1,0:T(8,128)(2,1)} async-done(((bf16[4,32,128,256]{3,2,1,0:T(8,128)(2,1)}), bf16[4,32,128,256]{3,2,1,0:T(8,128)(2,1)}, u32[]{:S(2)}, u32[]{:S(2)}) %all-to-all-start) | async-done | bytes 8388640 | tf_op jit(solution)/shard_map/all_to_all | solution.py:11
  198.8 4.9 %convert_reduce_fusion = bf16[32,128,256]{2,1,0:T(8,128)(2,1)S(1)} fusion(bf16[4,32,128,256]{3,2,1,0:T(8,128)(2,1)} %all-to-all-done), kind=kLoop, calls=%fused_computation.4 | loop fusion | flops 7340032 | bytes 10485760 | tf_op jit(solution)/shard_map/reduce_sum | solution.py:15
  203.7 0.0 all-gather.5.cloned.1.call-done
  203.8 11.4 %convolution_convert_fusion = bf16[32,128,1024]{2,1,0:T(8,128)(2,1)} fusion(bf16[32,256,1024]{2,1,0:T(8,128)(2,1)} %all-gather.5.cloned.1.call-done, bf16[32,128,256]{2,1,0:T(8,128)(2,1)S(1)} %convert_reduce_fusion), kind=kOutput, calls=%fused_computation.10 | convolution fusion | flops 2154823680 | bytes 27262976 | tf_op jit(solution)/shard_map/ncb,nbd->ncd/dot_general | solution.py:87
  215.1 15.4 %gather_fusion.1 = bf16[2048,1024]{1,0:T(8,128)(2,1)} fusion(bf16[4096,1024]{1,0:T(8,128)(2,1)} %bitcast.51, s32[2048]{0:T(1024)S(1)} %broadcast_clamp_fusion), kind=kCustom, calls=%fused_computation.1 | custom fusion | bytes 8396800 | tf_op jit(solution)/shard_map/jit(_take)/gather | solution.py:93
  230.6 5.3 %fusion.8 = f32[256,1,8]{2,1,0:T(1,128)S(1)} fusion(bf16[2048,1024]{1,0:T(8,128)(2,1)} %gather_fusion.1, pred[256,8]{1,0:T(8,128)(4,1)S(1)} %copy.38, bf16[256,1024,1]{1,0,2:T(8,128)(2,1)S(1)} %bitcast.58), kind=kOutput, calls=%fused_computation.17 | convolution fusion | flops 6291456 | bytes 4728832 | tf_op jit(solution)/shard_map/rkd,rd->rk/dot_general | solution.py:99
  235.9 0.1 copy.45
  236.0 7.8 %all_to_all.20 = f32[4,256,8]{1,2,0:T(8,128)S(1)} all-to-all(f32[4,256,8]{1,2,0:T(8,128)S(1)} %broadcast_in_dim.98), channel_id=1, replica_groups=mesh['adapter'=32,'mp'=4] {'mp'}, dimensions={0} | all-to-all | bytes 65536 | tf_op jit(solution)/shard_map/all_to_all | solution.py:11
  243.8 0.1 copy.46
  244.0 5.8 %fusion.7 = f32[256,1,1024]{2,1,0:T(1,128)S(1)} fusion(f32[256,8,1]{1,2,0:T(1,128)S(1)} %copy.46, bf16[2048,1024]{1,0:T(8,128)(2,1)} %gather_fusion.1, pred[256,8]{1,0:T(8,128)(4,1)S(1)} %copy.38), kind=kOutput, calls=%fused_computation.16 | convolution fusion | flops 27262976 | bytes 5253120 | tf_op jit(solution)/shard_map/rk,rkd->rd/dot_general | solution.py:104
  249.8 1.1 fusion.16
  (18 shorter events, 0.2 us)
Async XLA Ops:
  6.5 77.9 %all-gather.3.cloned.1.call-start = ((), (), s32[]{:S(2)}) async-start(), calls=%async_computation.4 | async-start | bytes 17301504 | tf_op jit(solution)/shard_map/all_gather | solution.py:82
  7.3 196.5 %all-gather.5.cloned.1.call-start = ((), (), s32[]{:S(2)}) async-start(), calls=%async_computation.5 | async-start | bytes 17301504 | tf_op jit(solution)/shard_map/all_gather | solution.py:90
  13.9 7.0 %copy-start.1 = (s32[256,8]{0,1:T(8,128)S(1)}, s32[256,8]{0,1:T(8,128)}, u32[]{:S(2)}) copy-start(s32[256,8]{0,1:T(8,128)} %param.7) | copy-start | bytes 24580
  13.9 16.5 %copy-start = (bf16[256,1024]{1,0:T(8,128)(2,1)S(1)}, bf16[256,1024]{1,0:T(8,128)(2,1)}, u32[]{:S(2)}) copy-start(bf16[256,1024]{1,0:T(8,128)(2,1)} %param.6) | copy-start | bytes 1572868
  15.5 42.3 %all-to-all-start.1 = ((bf16[4,256,1024]{2,1,0:T(8,128)(2,1)}), bf16[4,256,1024]{2,1,0:T(8,128)(2,1)S(1)}, u32[]{:S(2)}, u32[]{:S(2)}) async-start(bf16[4,256,1024]{2,1,0:T(8,128)(2,1)} %bitcast.53), calls=%async_computation.1 | async-start | bytes 4194304 | tf_op jit(solution)/shard_map/all_to_all | solution.py:25
  59.9 34.3 %all-to-all-start.2 = ((bf16[4,256,1024]{1,2,0:T(8,128)(2,1)}), bf16[4,256,1024]{1,2,0:T(8,128)(2,1)}, u32[]{:S(2)}, u32[]{:S(2)}) async-start(bf16[4,256,1024]{1,2,0:T(8,128)(2,1)} %broadcast_in_dim.97), calls=%async_computation.2 | async-start | bytes 4194304 | tf_op jit(solution)/shard_map/all_to_all | solution.py:11
  98.4 100.4 %all-to-all-start = ((bf16[4,32,128,256]{3,2,1,0:T(8,128)(2,1)}), bf16[4,32,128,256]{3,2,1,0:T(8,128)(2,1)}, u32[]{:S(2)}, u32[]{:S(2)}) async-start(bf16[4,32,128,256]{3,2,1,0:T(8,128)(2,1)} %broadcast_in_dim.94), calls=%async_computation | async-start | bytes 16777216 | tf_op jit(solution)/shard_map/all_to_all | solution.py:11
Sparse Core Ops, SparseCore 0:
  9.6 74.8 all-gather.2
  86.7 71.8 all-gather.4
where the time goes:
time: 258 us
  waiting for transfers between devices  109 us (42%)
  local copies, waits for them, and re-layouts  59.5 us (23%)
  matrix products  44.6 us (17%)
  starting transfers between devices  16.1 us (6%)
  between operations  13.6 us (5%)
  blocking collectives  7.81 us (3%)
  other arithmetic  7.31 us (3%)
    all_to_all x2, waiting for transfers between devices, sent_to_all(): lax.all_to_all(jnp.broadcast_to(x[None], (size, *x.shape)), axis, 0, 0, t...  87.5 us
    all_gather x1, waiting for transfers between devices, per_device(): lax.all_gather(down_weight, 'adapter', axis=0, tiled=True)  19.8 us
    gather x1, local copies, waits for them, and re-layouts, per_device(): jnp.take(hidden, source_row, axis=0)  18.2 us
    gather x1, local copies, waits for them, and re-layouts, per_device(): jnp.take(returned.reshape(total_adapters * capacity, width_local), flat_s...  15.4 us
    dot_general x1, matrix products, per_device(): jnp.einsum('ncb,nbd->ncd', block, lax.all_gather(up_weight, 'adapter', ax...  11.4 us
    all_to_all x2, starting transfers between devices, sent_to_all(): lax.all_to_all(jnp.broadcast_to(x[None], (size, *x.shape)), axis, 0, 0, t...  10.6 us
    dot_general x1, matrix products, per_device(): jnp.einsum('ncd,ndb->ncb', block, lax.all_gather(down_weight, 'adapter',...  9.7 us
    scatter x1, local copies, waits for them, and re-layouts, per_device(): jnp.zeros((total_adapters * capacity,), jnp.bool_).at[flat_slot.reshape(-1)]  9.12 us
  transfers between devices with their start and end apart: 5, of which 2 were waited for; matrix products, arithmetic and copies ran while one was open for 28% of the time, Pallas kernels for 0%

commit v1 on v0

--- a/solution.py
+++ b/solution.py
@@ -4,6 +4,12 @@
 from jax.sharding import PartitionSpec as P
 
 D = 4096
+
+
+def gather_from_all(x, axis, dim):
+    size = lax.axis_size(axis)
+    repeats = [size if d == dim else 1 for d in range(x.ndim)]
+    return lax.all_to_all(jnp.tile(x, repeats), axis, split_axis=dim, concat_axis=dim, tiled=True)
 
 
 def sent_to_all(x, axis):
@@ -79,7 +85,7 @@
         jnp.einsum(
             "ncd,ndb->ncb",
             block,
-            lax.all_gather(down_weight, "adapter", axis=0, tiled=True),
+            gather_from_all(down_weight, "adapter", 0),
             preferred_element_type=jnp.float32,
         )
     )

time: 258 us -> 479 us (1.86)
  the two profiles are of different devices: /device:TPU:0 before, /device:TPU:28 now
where the time goes in v1:
time: 479 us; the launch traced here: 478 us
  waiting for transfers between devices  291 us (61%)
  local copies, waits for them, and re-layouts  64.6 us (13%)
  matrix products  44.5 us (9%)
  blocking collectives  39.2 us (8%)
  starting transfers between devices  17.9 us (4%)
  between operations  13.7 us (3%)
  other arithmetic  7.31 us (2%)
    all_to_all x1, waiting for transfers between devices, gather_from_all(): lax.all_to_all(jnp.tile(x, repeats), axis, split_axis=dim, concat_axis=di...  187 us
    all_to_all x2, waiting for transfers between devices, sent_to_all(): lax.all_to_all(jnp.broadcast_to(x[None], (size, *x.shape)), axis, 0, 0, t...  103 us
    all_to_all x1, blocking collectives, sent_and_summed(): parts = lax.all_to_all(split_up(x, dim, size), axis, 0, 0, tiled=True)  31.4 us
    gather x1, local copies, waits for them, and re-layouts, per_device(): jnp.take(hidden, source_row, axis=0)  18.2 us
    gather x1, local copies, waits for them, and re-layouts, per_device(): jnp.take(returned.reshape(total_adapters * capacity, width_local), flat_s...  15.4 us
    dot_general x1, matrix products, per_device(): jnp.einsum('ncb,nbd->ncd', block, lax.all_gather(up_weight, 'adapter', ax...  11.4 us
    all_to_all x2, starting transfers between devices, sent_to_all(): lax.all_to_all(jnp.broadcast_to(x[None], (size, *x.shape)), axis, 0, 0, t...  10.3 us
    dot_general x1, matrix products, per_device(): jnp.einsum('ncd,ndb->ncb', block, gather_from_all(down_weight, 'adapter',...  9.72 us
  transfers between devices with their start and end apart: 4, of which 3 were waited for; matrix products, arithmetic and copies ran while one was open for 16% of the time, Pallas kernels for 0%

profile of v1, /device:TPU:28, one launch (start us, length us, event | category | flops | bytes accessed | tf_op | source)
XLA Modules:
  0.0 478.0 jit_solution(7472549547056646404)
XLA Ops:
  6.5 0.0 all-gather.2.cloned.1.call-start
  6.5 0.7 all-gather.2.cloned.1.call-update
  7.3 5.9 %convolution_convert_fusion.1 = bf16[256,4096]{1,0:T(8,128)(2,1)S(1)} fusion(bf16[256,1024]{1,0:T(8,128)(2,1)} %param.6, bf16[1024,4096]{1,0:T(8,128)(2,1)} %param.10), kind=kOutput, calls=%fused_computation.11 | convolution fusion | flops 2148532224 | bytes 11010048 | tf_op jit(solution)/shard_map/dot_general | solution.py:77
  13.2 0.0 copy-start.1
  13.2 0.2 copy.58
  13.4 31.4 %all_to_all.25 = bf16[4,256,1024]{2,1,0:T(8,128)(2,1)S(1)} all-to-all(bf16[4,256,1024]{2,1,0:T(8,128)(2,1)S(1)} %bitcast.54), channel_id=1, replica_groups=mesh['adapter'=32,'mp'=4] {'mp'}, dimensions={0} | all-to-all | bytes 4194304 | tf_op jit(solution)/shard_map/all_to_all | solution.py:31
  44.8 0.0 copy-done.1
  44.8 6.5 %tile.10 = bf16[32,1024,256]{2,1,0:T(8,128)(2,1)} broadcast(bf16[1024,256]{1,0:T(8,128)(2,1)S(1)} %bitcast.56), dimensions={1,2} | broadcast | bytes 17301504 | tf_op jit(solution)/shard_map/tile | solution.py:12
  51.2 0.0 copy-start.2
  51.3 7.6 %all-to-all-start = ((bf16[32,1024,256]{2,1,0:T(8,128)(2,1)}), bf16[32,1024,256]{2,1,0:T(8,128)(2,1)}, u32[]{:S(2)}, u32[]{:S(2)}) async-start(bf16[32,1024,256]{2,1,0:T(8,128)(2,1)} %tile.10), calls=%async_computation | async-start | bytes 33554432 | tf_op jit(solution)/shard_map/all_to_all | solution.py:12
  58.8 0.0 copy-done.2
  58.9 0.0 copy-start
  58.9 0.6 reduce-window.6
  59.5 0.2 slice_reduce_fusion
  59.7 0.1 fusion.18
  59.8 0.1 select_reduce_fusion
  59.9 0.1 copy.39
  60.0 0.1 reshape.90
  60.2 0.1 reshape.123
  60.3 8.1 %scatter_custom_fusion.1 = s32[4096]{0:T(1024)S(1)} fusion(s32[2048]{0:T(1024)S(1)} %bitcast.57, s32[2048]{0:T(1024)S(1)} %reshape.123, s32[]{:T(128)} %constant.18.clone.1), kind=kCustom, calls=%fused_computation.45 | custom fusion | bytes 16388 | tf_op jit(solution)/shard_map/scatter | solution.py:70
  68.4 0.0 copy-done
  68.4 18.2 %gather_fusion = bf16[4096,1024]{1,0:T(8,128)(2,1)} fusion(bf16[256,1024]{1,0:T(8,128)(2,1)S(1)} %copy-done, s32[4096]{0:T(1024)S(1)} %fusion.19), kind=kCustom, calls=%fused_computation | custom fusion | bytes 16793600 | tf_op jit(solution)/shard_map/jit(_take)/gather | solution.py:74
  86.6 9.1 %scatter_custom_fusion = pred[4096]{0:T(1024)(128)(4,1)S(1)} fusion(s32[2048]{0:T(1024)S(1)} %bitcast.58, pred[2048]{0:T(1024)(128)(4,1)S(1)} %broadcast.52, pred[]{:T(512)} %constant.27.clone.1), kind=kCustom, calls=%fused_computation.48 | custom fusion | bytes 4097 | tf_op jit(solution)/shard_map/scatter | solution.py:72
  95.7 0.4 reduce_sum.69
  96.2 0.2 copy.43
  96.4 187.0 %all-to-all-done = bf16[32,1024,256]{2,1,0:T(8,128)(2,1)} async-done(((bf16[32,1024,256]{2,1,0:T(8,128)(2,1)}), bf16[32,1024,256]{2,1,0:T(8,128)(2,1)}, u32[]{:S(2)}, u32[]{:S(2)}) %all-to-all-start) | async-done | bytes 16777248 | tf_op jit(solution)/shard_map/all_to_all | solution.py:12
  283.4 1.5 broadcast_in_dim.97
  284.9 4.6 all-to-all-start.3
  289.5 9.7 %fusion.12 = bf16[32,128,256]{2,1,0:T(8,128)(2,1)S(1)} fusion(bf16[32,1024,256]{2,1,0:T(8,128)(2,1)} %all-to-all-done, bf16[32,128,1024]{2,1,0:T(8,128)(2,1)} %bitcast.53, pred[32,128]{1,0:T(8,128)(4,1)S(1)} %and_bitcast_fusion, pred[32,128]{1,0:T(8,128)(4,1)S(1)} %bitcast.59), kind=kOutput, calls=%fused_computation.22 | convolution fusion | flops 2156920832 | bytes 27271168 | tf_op jit(solution)/shard_map/ncd,ndb->ncb/dot_general | solution.py:85
  299.2 17.1 %all-to-all-done.3 = bf16[4,256,1024]{1,2,0:T(8,128)(2,1)} async-done(((bf16[4,256,1024]{1,2,0:T(8,128)(2,1)}), bf16[4,256,1024]{1,2,0:T(8,128)(2,1)}, u32[]{:S(2)}, u32[]{:S(2)}) %all-to-all-start.3) | async-done | bytes 2097184 | tf_op jit(solution)/shard_map/all_to_all | solution.py:17
  316.4 4.3 broadcast_in_dim.94
  320.6 5.7 %all-to-all-start.1 = ((bf16[4,32,128,256]{3,2,1,0:T(8,128)(2,1)}), bf16[4,32,128,256]{3,2,1,0:T(8,128)(2,1)}, u32[]{:S(2)}, u32[]{:S(2)}) async-start(bf16[4,32,128,256]{3,2,1,0:T(8,128)(2,1)} %broadcast_in_dim.94), calls=%async_computation.1 | async-start | bytes 16777216 | tf_op jit(solution)/shard_map/all_to_all | solution.py:17
  326.3 0.1 copy.40
  326.4 0.1 reshape.105
  326.5 0.2 copy.38
  326.7 6.5 %fusion.15 = (f32[256]{0:T(256)S(1)}, bf16[256,1024]{1,0:T(8,128)(2,1)S(1)}) fusion(bf16[256,1024]{1,0:T(8,128)(2,1)S(1)} %copy-done, bf16[256,4096]{0,1:T(8,128)(2,1)} %bitcast.11, bf16[1024,4096]{1,0:T(8,128)(2,1)} %param.11), kind=kOutput, calls=%fused_computation.26 | convolution fusion | flops 2148794112 | bytes 11535360 | tf_op jit(solution)/shard_map/dot_general | solution.py:80
  333.2 86.0 %all-to-all-done.1 = bf16[4,32,128,256]{3,2,1,0:T(8,128)(2,1)} async-done(((bf16[4,32,128,256]{3,2,1,0:T(8,128)(2,1)}), bf16[4,32,128,256]{3,2,1,0:T(8,128)(2,1)}, u32[]{:S(2)}, u32[]{:S(2)}) %all-to-all-start.1) | async-done | bytes 8388640 | tf_op jit(solution)/shard_map/all_to_all | solution.py:17
  419.2 4.9 %convert_reduce_fusion = bf16[32,128,256]{2,1,0:T(8,128)(2,1)S(1)} fusion(bf16[4,32,128,256]{3,2,1,0:T(8,128)(2,1)} %all-to-all-done.1), kind=kLoop, calls=%fused_computation.4 | loop fusion | flops 7340032 | bytes 10485760 | tf_op jit(solution)/shard_map/reduce_sum | solution.py:21
  424.1 0.0 all-gather.2.cloned.1.call-done
  424.1 11.4 %convolution_convert_fusion = bf16[32,128,1024]{2,1,0:T(8,128)(2,1)} fusion(bf16[32,256,1024]{2,1,0:T(8,128)(2,1)} %all-gather.2.cloned.1.call-done, bf16[32,128,256]{2,1,0:T(8,128)(2,1)S(1)} %convert_reduce_fusion), kind=kOutput, calls=%fused_computation.10 | convolution fusion | flops 2154823680 | bytes 27262976 | tf_op jit(solution)/shard_map/ncb,nbd->ncd/dot_general | solution.py:93
  435.5 15.4 %gather_fusion.1 = bf16[2048,1024]{1,0:T(8,128)(2,1)} fusion(bf16[4096,1024]{1,0:T(8,128)(2,1)} %bitcast.52, s32[2048]{0:T(1024)S(1)} %broadcast_clamp_fusion), kind=kCustom, calls=%fused_computation.1 | custom fusion | bytes 8396800 | tf_op jit(solution)/shard_map/jit(_take)/gather | solution.py:99
  450.9 5.3 %fusion.8 = f32[256,1,8]{2,1,0:T(1,128)S(1)} fusion(bf16[2048,1024]{1,0:T(8,128)(2,1)} %gather_fusion.1, pred[256,8]{1,0:T(8,128)(4,1)S(1)} %copy.38, bf16[256,1024,1]{1,0,2:T(8,128)(2,1)S(1)} %bitcast.60), kind=kOutput, calls=%fused_computation.17 | convolution fusion | flops 6291456 | bytes 4728832 | tf_op jit(solution)/shard_map/rkd,rd->rk/dot_general | solution.py:105
  456.2 0.1 copy.45
  456.3 7.8 %all_to_all.26 = f32[4,256,8]{1,2,0:T(8,128)S(1)} all-to-all(f32[4,256,8]{1,2,0:T(8,128)S(1)} %broadcast_in_dim.98), channel_id=1, replica_groups=mesh['adapter'=32,'mp'=4] {'mp'}, dimensions={0} | all-to-all | bytes 65536 | tf_op jit(solution)/shard_map/all_to_all | solution.py:17
  464.2 0.1 copy.46
  464.3 5.8 %fusion.7 = f32[256,1,1024]{2,1,0:T(1,128)S(1)} fusion(f32[256,8,1]{1,2,0:T(1,128)S(1)} %copy.46, bf16[2048,1024]{1,0:T(8,128)(2,1)} %gather_fusion.1, pred[256,8]{1,0:T(8,128)(4,1)S(1)} %copy.38), kind=kOutput, calls=%fused_computation.16 | convolution fusion | flops 27262976 | bytes 5253120 | tf_op jit(solution)/shard_map/rk,rkd->rd/dot_general | solution.py:110
  470.1 1.1 fusion.16
  (18 shorter events, 0.2 us)
Async XLA Ops:
  6.5 417.6 %all-gather.2.cloned.1.call-start = ((), (), s32[]{:S(2)}) async-start(), calls=%async_computation.5 | async-start | bytes 17301504 | tf_op jit(solution)/shard_map/all_gather | solution.py:96
  13.2 31.6 %copy-start.1 = (bf16[1,1024,256]{2,1,0:T(8,128)(2,1)S(1)}, bf16[1,1024,256]{2,1,0:T(8,128)(2,1)}, u32[]{:S(2)}) copy-start(bf16[1,1024,256]{2,1,0:T(8,128)(2,1)} %param.8) | copy-start | bytes 1572868
  51.2 7.6 %copy-start.2 = (s32[256,8]{0,1:T(8,128)S(1)}, s32[256,8]{0,1:T(8,128)}, u32[]{:S(2)}) copy-start(s32[256,8]{0,1:T(8,128)} %param.7) | copy-start | bytes 24580
  51.3 232.1 %all-to-all-start = ((bf16[32,1024,256]{2,1,0:T(8,128)(2,1)}), bf16[32,1024,256]{2,1,0:T(8,128)(2,1)}, u32[]{:S(2)}, u32[]{:S(2)}) async-start(bf16[32,1024,256]{2,1,0:T(8,128)(2,1)} %tile.10), calls=%async_computation | async-start | bytes 33554432 | tf_op jit(solution)/shard_map/all_to_all | solution.py:12
  58.9 9.5 %copy-start = (bf16[256,1024]{1,0:T(8,128)(2,1)S(1)}, bf16[256,1024]{1,0:T(8,128)(2,1)}, u32[]{:S(2)}) copy-start(bf16[256,1024]{1,0:T(8,128)(2,1)} %param.6) | copy-start | bytes 1572868
  284.9 31.5 %all-to-all-start.3 = ((bf16[4,256,1024]{1,2,0:T(8,128)(2,1)}), bf16[4,256,1024]{1,2,0:T(8,128)(2,1)}, u32[]{:S(2)}, u32[]{:S(2)}) async-start(bf16[4,256,1024]{1,2,0:T(8,128)(2,1)} %broadcast_in_dim.97), calls=%async_computation.3 | async-start | bytes 4194304 | tf_op jit(solution)/shard_map/all_to_all | solution.py:17
  320.6 98.6 %all-to-all-start.1 = ((bf16[4,32,128,256]{3,2,1,0:T(8,128)(2,1)}), bf16[4,32,128,256]{3,2,1,0:T(8,128)(2,1)}, u32[]{:S(2)}, u32[]{:S(2)}) async-start(bf16[4,32,128,256]{3,2,1,0:T(8,128)(2,1)} %broadcast_in_dim.94), calls=%async_computation.1 | async-start | bytes 16777216 | tf_op jit(solution)/shard_map/all_to_all | solution.py:17
Sparse Core Ops, SparseCore 0:
  9.6 194.5 all-gather.1
